TPU v7x, 32 devices: a whole 2x2x4 slice. The times are simulated.
32 devices in a mesh: row: 4 (over z), replica: 4 (over y, core), feat: 2 (over x).
Axes of the slice: x: 2, y: 2, z: 4, core: 2. Of those that a mesh axis runs over, the one named last changes fastest.
Arguments:
- features: bfloat16 [4, 4096, 256], P('replica', ('row', 'feat')), may hold values from -6 to 6
- tiles: bfloat16 [4, 32, 4, 3, 128, 128], P('replica', ('row', 'feat')), may hold values from 0 to 1
- block_cols: int32 [4, 32, 4, 3], P('replica', ('row', 'feat')), may hold values from 0 to 7
- block_counts: int32 [4, 32, 4], P('replica', ('row', 'feat')), may hold values from 0 to 3, as said below
- degrees: int32 [4, 4096], P('replica', ('row', 'feat')), may hold values from 32 to 287
- w_self: bfloat16 [256, 256], P(None, 'feat'), may hold values from -0.375 to 0.375
- w_neigh: bfloat16 [256, 256], P(None, 'feat'), may hold values from -0.375 to 0.375
- gamma: float32 [256], P('feat'), may hold values from 0.5 to 1.5
- beta: float32 [256], P('feat'), may hold values from -3 to 3
Outputs:
- hidden_out: bfloat16 [4, 4096, 256], P('replica', 'row', 'feat')
Inputs may be any that keep to these rules, and one draw needn't show every extreme that they name: `block_counts`: some block row uses all 3 slots of some source shard in every partition.
All inputs are finite; a program needn't handle non-finite values.
Results may differ from a plain program's by a relative error of at most 0.001.
Values may be sent and summed in bfloat16 or wider, within the bound.
No kernel may reach another device: no remote copies, remote signals or barrier semaphores. Data moves between devices by JAX's collectives and lax.ppermute only.
A program may use at most 128 MiB of HBM per device.

v0:
```python
import jax
import jax.numpy as jnp
from jax import lax
from jax.sharding import PartitionSpec as P


def per_device(features, tiles, block_cols, block_counts, degrees, w_self, w_neigh, gamma, beta):
    local_x = features[0]
    local_tiles = tiles[0]
    local_cols = block_cols[0]
    local_counts = block_counts[0]
    nodes_here = local_x.shape[0]
    width = local_x.shape[1]
    block_size = local_tiles.shape[3]
    slots = local_tiles.shape[2]
    row_blocks = local_tiles.shape[0]
    pair = lax.all_gather(local_x, "feat", axis=0, tiled=True)
    shard_rows = pair.shape[0]
    shard_blocks = shard_rows // block_size
    slot_index = jnp.arange(slots, dtype=jnp.int32)[None, :]
    start_total = jnp.zeros((row_blocks, block_size, width), jnp.float32)
    piece = lax.all_gather(pair, "row", axis=0, tiled=True)
    count_shards = piece.shape[0] // shard_rows
    shards = piece.reshape(count_shards, shard_blocks, block_size, width)

    def one_shard(step, acc):
        shard = lax.dynamic_index_in_dim(shards, step, 0, keepdims=False)
        counts_now = lax.dynamic_index_in_dim(local_counts, step, 1, keepdims=False)
        cols_now = lax.dynamic_index_in_dim(local_cols, step, 1, keepdims=False)
        tiles_now = lax.dynamic_index_in_dim(local_tiles, step, 1, keepdims=False)
        picked = shard[cols_now]
        used = slot_index < counts_now[:, None]
        masked = jnp.where(used[:, :, None, None], tiles_now, jnp.zeros((), tiles_now.dtype))
        return acc + jnp.einsum(
            "bcij,bcjf->bif", masked, picked, preferred_element_type=jnp.float32
        )

    agg_sum = lax.fori_loop(0, count_shards, one_shard, start_total).reshape(nodes_here, width)
    agg = (agg_sum / degrees[0][:, None].astype(jnp.float32)).astype(jnp.bfloat16)
    agg_pair = lax.all_gather(agg, "feat", axis=0, tiled=True)
    pre = jnp.dot(pair, w_self, preferred_element_type=jnp.float32) + jnp.dot(
        agg_pair, w_neigh, preferred_element_type=jnp.float32
    )
    col_sum, col_sq = lax.psum(
        (jnp.sum(pre, axis=0), jnp.sum(pre * pre, axis=0)), ("row", "replica")
    )
    total_nodes = pre.shape[0] * lax.axis_size("row") * lax.axis_size("replica")
    mean = col_sum / total_nodes
    var = col_sq / total_nodes - mean * mean
    normed = gamma * (pre - mean) / jnp.sqrt(var + 1e-05) + beta
    return jnp.maximum(normed, 0.0).astype(jnp.bfloat16)[None]


def solution(mesh):
    in_specs = (
        P("replica", ("row", "feat"), None),
        P("replica", ("row", "feat"), None, None, None, None),
        P("replica", ("row", "feat"), None, None),
        P("replica", ("row", "feat"), None),
        P("replica", ("row", "feat")),
        P(None, "feat"),
        P(None, "feat"),
        P("feat"),
        P("feat"),
    )
    out_specs = P("replica", "row", "feat")
    return jax.shard_map(
        per_device, mesh=mesh, in_specs=in_specs, out_specs=out_specs, check_vma=False
    )
```

profile of v0, /device:TPU:0, one launch (start us, length us, event | category | flops | bytes accessed | tf_op | source)
XLA Modules:
  0.0 121.8 jit_solution(17375432722191585981)
XLA Ops:
  6.5 0.0 copy-start
  6.5 0.0 all-gather.4.cloned.1.call-start
  6.5 12.0 %all-gather = bf16[1,1024,256]{2,1,0:T(8,128)(2,1)} all-gather(bf16[1,512,256]{2,1,0:T(8,128)(2,1)} %param.11), channel_id=2, replica_groups=mesh['row'=4,'replica'=4,'feat'=2] {'feat'}, dimensions={1}, use_global_device_ids=true | all-gather | bytes 786432 | tf_op jit(solution)/shard_map/all_gather | solution.py:17
  18.6 0.0 all-gather.4.cloned.1.call-update
  18.6 0.0 copy-start.4
  18.6 0.0 copy-start.5
  18.6 0.0 copy-start.6
  18.6 0.0 copy-start.1
  18.7 0.0 copy-start.3
  18.7 1.6 %copy.20 = bf16[1,4,4,3,128,128]{5,4,3,1,2,0:T(8,128)(2,1)S(1)} copy(bf16[1,4,4,3,128,128]{5,4,3,2,1,0:T(8,128)(2,1)} %param.12) | data formatting | bytes 3145728 | tf_op args[1]
  20.2 0.0 copy-done.4
  20.3 0.1 copy.17
  20.4 0.0 copy-done.5
  20.4 0.1 copy.16
  20.5 0.0 copy-done.6
  20.5 0.0 copy-done.1
  20.5 0.0 copy-done.3
  20.5 1.1 fusion.10
  21.6 43.2 %all-gather.4.cloned.1.call-done = bf16[1,4096,256]{2,1,0:T(8,128)(2,1)} async-done(((bf16[1,1024,256]{2,1,0:T(8,128)(2,1)}), bf16[1,4096,256]{2,1,0:T(8,128)(2,1)}) %all-gather.4.cloned.1.call-update) | async-done | bytes 2097168 | tf_op jit(solution)/shard_map/all_gather | solution.py:22
  64.7 9.8 %while.14 = (s32[]{:T(128)}, f32[4,128,256]{2,1,0:T(8,128)S(1)}, s32[4,4]{0,1:T(4,128)S(1)}, bf16[4,4,3,128,128]{4,3,2,0,1:T(8,128)(2,1)S(1)}, bf16[4,8,128,256]...) while((s32[]{:T(128)}, f32[4,128,256]{2,1,0:T(8,128)S(1)}, ...), condition=%wide.region_1.2_spmd.clone, body=%wide.region_0.1_spmd.clone.sunk | while | flops 101123120 | bytes 4854827 | solution.py:38
  64.7 1.1 dynamic-slice_bitcast_fusion.2
  65.8 0.1 copy.22
  65.9 0.1 reshape.106
  66.0 0.6 gather_fusion
  66.6 0.1 iota_compare_fusion.2
  66.7 0.4 fusion.23
  67.2 1.1 dynamic-slice_bitcast_fusion.2
  68.3 0.1 copy.22
  68.4 0.1 reshape.106
  68.5 0.6 gather_fusion
  69.1 0.1 iota_compare_fusion.2
  69.2 0.4 fusion.23
  69.6 1.1 dynamic-slice_bitcast_fusion.2
  70.7 0.1 copy.22
  70.8 0.1 reshape.106
  70.9 0.6 gather_fusion
  71.5 0.1 iota_compare_fusion.2
  71.6 0.4 fusion.23
  72.1 1.1 dynamic-slice_bitcast_fusion.2
  73.2 0.1 copy.22
  73.2 0.1 reshape.106
  73.3 0.6 gather_fusion
  74.0 0.1 iota_compare_fusion.2
  74.0 0.4 fusion.23
  74.5 0.0 copy-start.2
  74.5 0.0 copy-start.7
  74.5 0.0 copy-start.8
  74.5 0.1 fusion.9
  74.7 8.6 %all_gather.11 = bf16[1024,256]{1,0:T(8,128)(2,1)S(1)} all-gather(bf16[512,256]{1,0:T(8,128)(2,1)S(1)} %fusion.9), channel_id=1, replica_groups=mesh['row'=4,'replica'=4,'feat'=2] {'feat'}, dimensions={0}, use_global_device_ids=true | all-gather | bytes 786432 | tf_op jit(solution)/shard_map/all_gather | solution.py:40
  83.2 0.0 copy-done
  83.2 0.0 copy-done.2
  83.2 0.4 fusion.13
  83.6 30.5 %all-reduce = (f32[128]{0:T(128)S(1)}, f32[128]{0:T(128)S(1)}) all-reduce(f32[128]{0:T(128)S(1)} %get-tuple-element.166, f32[128]{0:T(128)S(1)} %get-tuple-element.165), channel_id=1, replica_groups=mesh['row'=4,'replica'=4,'feat'=2] {'row','replica'}, use_global_device_ids=true, to_apply=%region_5.6 | all-reduce | flops 256 | bytes 2048 | tf_op jit(solution)/shard_map/psum | solution.py:44
  114.2 0.0 copy-done.7
  114.2 0.0 copy-done.8
  114.2 0.8 fusion.12
  (15 shorter events, 0.1 us)
Async XLA Ops:
  6.5 76.7 %copy-start = (bf16[256,128]{1,0:T(8,128)(2,1)S(1)}, bf16[256,128]{1,0:T(8,128)(2,1)}, u32[]{:S(2)}) copy-start(bf16[256,128]{1,0:T(8,128)(2,1)} %param.17) | copy-start | bytes 196612
  6.5 58.2 %all-gather.4.cloned.1.call-start = ((), (), s32[]{:S(2)}) async-start(), calls=%async_computation | async-start | bytes 2621440 | tf_op jit(solution)/shard_map/all_gather | solution.py:22
  18.6 1.6 %copy-start.4 = (s32[1,4,4,3]{2,1,3,0:T(4,128)S(1)}, s32[1,4,4,3]{2,1,3,0:T(4,128)}, u32[]{:S(2)}) copy-start(s32[1,4,4,3]{2,1,3,0:T(4,128)} %param.13) | copy-start | bytes 580
  18.6 1.7 %copy-start.5 = (s32[1,4,4]{2,1,0:T(4,128)S(1)}, s32[1,4,4]{2,1,0:T(4,128)}, u32[]{:S(2)}) copy-start(s32[1,4,4]{2,1,0:T(4,128)} %param.14) | copy-start | bytes 196
  18.6 1.8 %copy-start.6 = (s32[1,512]{1,0:T(1,128)S(1)}, s32[1,512]{1,0:T(1,128)}, u32[]{:S(2)}) copy-start(s32[1,512]{1,0:T(1,128)} %param.15) | copy-start | bytes 6148
  18.6 1.8 %copy-start.1 = (bf16[1,1024,256]{2,1,0:T(8,128)(2,1)S(1)}, bf16[1,1024,256]{2,1,0:T(8,128)(2,1)}, u32[]{:S(2)}) copy-start(bf16[1,1024,256]{2,1,0:T(8,128)(2,1)} %all-gather) | copy-start | bytes 1572868
  18.7 1.8 %copy-start.3 = (bf16[256,128]{1,0:T(8,128)(2,1)S(1)}, bf16[256,128]{1,0:T(8,128)(2,1)}, u32[]{:S(2)}) copy-start(bf16[256,128]{1,0:T(8,128)(2,1)} %param.16) | copy-start | bytes 196612
  74.5 8.7 %copy-start.2 = (f32[1024,128]{1,0:T(8,128)S(1)}, f32[1024,128]{1,0:T(8,128)}, u32[]{:S(2)}) copy-start(f32[1024,128]{1,0:T(8,128)} %fusion.10) | copy-start | bytes 1572868
  74.5 39.7 %copy-start.7 = (f32[128]{0:T(128)S(1)}, f32[128]{0:T(128)}, u32[]{:S(2)}) copy-start(f32[128]{0:T(128)} %param.19) | copy-start | bytes 1540
  74.5 39.7 %copy-start.8 = (f32[128]{0:T(128)S(1)}, f32[128]{0:T(128)}, u32[]{:S(2)}) copy-start(f32[128]{0:T(128)} %param.18) | copy-start | bytes 1540
Sparse Core Ops, SparseCore 0:
  18.7 45.9 all-gather.3
where the time goes:
time: 122 us
  blocking collectives  51.1 us (42%)
  waiting for transfers between devices  43.2 us (35%)
  between operations  13.5 us (11%)
  local copies, waits for them, and re-layouts  9.28 us (8%)
  matrix products  3.2 us (3%)
  other arithmetic  1.35 us (1%)
    all_gather x1, waiting for transfers between devices, per_device(): piece = lax.all_gather(pair, 'row', axis=0, tiled=True)  43.2 us
    psum x1, blocking collectives, per_device(): lax.psum((jnp.sum(pre, axis=0), jnp.sum(pre * pre, axis=0)), ('row', 'rep...  30.5 us
    all_gather x1, blocking collectives, per_device(): pair = lax.all_gather(local_x, 'feat', axis=0, tiled=True)  12 us
    all_gather x1, blocking collectives, per_device(): agg_pair = lax.all_gather(agg, 'feat', axis=0, tiled=True)  8.55 us
    squeeze x4, local copies, waits for them, and re-layouts, one_shard(): shard = lax.dynamic_index_in_dim(shards, step, 0, keepdims=False)  4.32 us
  transfers between devices with their start and end apart: 1, of which 1 were waited for; matrix products, arithmetic and copies ran while one was open for 2% of the time, Pallas kernels for 0%

commit v1 on v0

--- a/solution.py
+++ b/solution.py
@@ -2,6 +2,23 @@
 import jax.numpy as jnp
 from jax import lax
 from jax.sharding import PartitionSpec as P
+
+
+def joined_along(tiles, dim):
+    dims = list(tiles.shape[1:])
+    dims[dim] *= tiles.shape[0]
+    return jnp.moveaxis(tiles, 0, dim).reshape(dims)
+
+
+def gather_around(value, axis, dim):
+    count = lax.axis_size(axis)
+    right = [(i, (i + 1) % count) for i in range(count)]
+    pieces = [value]
+    while len(pieces) < count:
+        pieces.append(lax.ppermute(pieces[-1], axis, right))
+    index = lax.axis_index(axis)
+    pieces = jnp.stack(pieces)[(index - jnp.arange(count)) % count]
+    return joined_along(pieces, dim)
 
 
 def per_device(features, tiles, block_cols, block_counts, degrees, w_self, w_neigh, gamma, beta):
@@ -19,7 +36,7 @@
     shard_blocks = shard_rows // block_size
     slot_index = jnp.arange(slots, dtype=jnp.int32)[None, :]
     start_total = jnp.zeros((row_blocks, block_size, width), jnp.float32)
-    piece = lax.all_gather(pair, "row", axis=0, tiled=True)
+    piece = gather_around(pair, "row", 0)
     count_shards = piece.shape[0] // shard_rows
     shards = piece.reshape(count_shards, shard_blocks, block_size, width)
 

time: 122 us -> 109 us (0.89)
  between operations: 13.5 us -> 0.09 us
  waiting for transfers between devices: 43.2 us -> 36 us
  local copies, waits for them, and re-layouts: 9.28 us -> 13.5 us
  blocking collectives: 51.1 us -> 46.9 us
  matrix products: 3.2 us -> 7.18 us
  starting transfers between devices: 0.01 us -> 1.78 us
  other arithmetic: 1.35 us -> 2.99 us
    all_gather x1 -> x0, waiting for transfers between devices: 43.2 us -> none  [per_device(): piece = lax.all_gather(pair, 'row', axis=0, tiled=True)]
    ppermute x0 -> x3, waiting for transfers between devices: none -> 36 us  [gather_around(): pieces.append(lax.ppermute(pieces[-1], axis, right))]
    dot_general x4, matrix products: 1.73 us -> 5.71 us  [one_shard(): jnp.einsum('bcij,bcjf->bif', masked, picked, preferred_element_type=jnp.f...]
    unnamed x21 -> x25, local copies, waits for them, and re-layouts: 1.82 us -> 3.99 us
    gather x0 -> x1, local copies, waits for them, and re-layouts: none -> 2.02 us  [gather_around(): pieces = jnp.stack(pieces)[(index - jnp.arange(count)) % count]]
    ppermute x0 -> x3, starting transfers between devices: none -> 1.78 us  [gather_around(): pieces.append(lax.ppermute(pieces[-1], axis, right))]
    all_gather x1, blocking collectives: 12 us -> 10.3 us  [per_device(): pair = lax.all_gather(local_x, 'feat', axis=0, tiled=True)]
    another operation x0 -> x1, other arithmetic: none -> 1.62 us  [gather_around(): pieces = jnp.stack(pieces)[(index - jnp.arange(count)) % count]]
  transfers between devices with their start and end apart: 1 -> 3, of which waited for: 1 -> 3; matrix products, arithmetic and copies ran while one was open for 2% -> 4% of each run, Pallas kernels for 0% -> 0%
where the time goes in v1:
time: 109 us
  blocking collectives  46.9 us (43%)
  waiting for transfers between devices  36 us (33%)
  local copies, waits for them, and re-layouts  13.5 us (12%)
  matrix products  7.18 us (7%)
  other arithmetic  2.99 us (3%)
  starting transfers between devices  1.78 us (2%)
    ppermute x3, waiting for transfers between devices, gather_around(): pieces.append(lax.ppermute(pieces[-1], axis, right))  36 us
    psum x1, blocking collectives, per_device(): lax.psum((jnp.sum(pre, axis=0), jnp.sum(pre * pre, axis=0)), ('row', 'rep...  29.5 us
    all_gather x1, blocking collectives, per_device(): pair = lax.all_gather(local_x, 'feat', axis=0, tiled=True)  10.3 us
    all_gather x1, blocking collectives, per_device(): agg_pair = lax.all_gather(agg, 'feat', axis=0, tiled=True)  7.04 us
    dot_general x4, matrix products, one_shard(): jnp.einsum('bcij,bcjf->bif', masked, picked, preferred_element_type=jnp.f...  5.71 us
    squeeze x4, local copies, waits for them, and re-layouts, one_shard(): shard = lax.dynamic_index_in_dim(shards, step, 0, keepdims=False)  4.37 us
    unnamed x25, local copies, waits for them, and re-layouts  3.99 us
    gather x4, local copies, waits for them, and re-layouts, one_shard(): picked = shard[cols_now]  2.39 us
  transfers between devices with their start and end apart: 3, of which 3 were waited for; matrix products, arithmetic and copies ran while one was open for 4% of the time, Pallas kernels for 0%

profile of v1, /device:TPU:0, one launch (start us, length us, event | category | flops | bytes accessed | tf_op | source)
XLA Modules:
  0.0 108.7 jit_solution(16725656005644445213)
XLA Ops:
  0.0 0.0 copy-start
  0.0 0.0 copy-start.6
  0.0 0.0 copy-start.7
  0.0 0.0 copy-start.8
  0.0 0.0 copy-start.5
  0.0 10.3 %all-gather = bf16[1,1024,256]{2,1,0:T(8,128)(2,1)S(1)} all-gather(bf16[1,512,256]{2,1,0:T(8,128)(2,1)} %param.11), channel_id=2, replica_groups=mesh['row'=4,'replica'=4,'feat'=2] {'feat'}, dimensions={1}, use_global_device_ids=true | all-gather | bytes 786432 | tf_op jit(solution)/shard_map/all_gather | solution.py:34
  10.4 1.8 %collective-permute-start = (bf16[1024,256]{1,0:T(8,128)(2,1)S(1)}, bf16[1024,256]{1,0:T(8,128)(2,1)S(1)}, u32[]{:S(2)}, u32[]{:S(2)}) collective-permute-start(bf16[1024,256]{1,0:T(8,128)(2,1)S(1)} %bitcast.59), channel_id=1, source_target_pairs={{0,8},{8,16},{16,24},{24,0},{1,9},{9,17},{17,25},{25,1},{2,10},{10... | collective-permute-start | bytes 1572872 | tf_op jit(solution)/shard_map/ppermute | solution.py:18
  12.1 13.1 %collective-permute-done = bf16[1024,256]{1,0:T(8,128)(2,1)S(1)} collective-permute-done((bf16[1024,256]{1,0:T(8,128)(2,1)S(1)}, bf16[1024,256]{1,0:T(8,128)(2,1)S(1)}, u32[]{:S(2)}, u32[]{:S(2)}) %collective-permute-start) | collective-permute-done | bytes 524320 | tf_op jit(solution)/shard_map/ppermute | solution.py:18
  25.3 0.0 copy-start.2
  25.3 0.0 collective-permute-start.1
  25.3 14.0 %collective-permute-done.1 = bf16[1024,256]{1,0:T(8,128)(2,1)S(1)} collective-permute-done((bf16[1024,256]{1,0:T(8,128)(2,1)S(1)}, bf16[1024,256]{1,0:T(8,128)(2,1)S(1)}, u32[]{:S(2)}, u32[]{:S(2)}) %collective-permute-start.1) | collective-permute-done | bytes 524320 | tf_op jit(solution)/shard_map/ppermute | solution.py:18
  39.3 0.0 copy-start.3
  39.3 0.0 collective-permute-start.2
  39.3 2.9 %copy.20 = bf16[1,4,4,3,128,128]{5,4,3,1,2,0:T(8,128)(2,1)} copy(bf16[1,4,4,3,128,128]{5,4,3,2,1,0:T(8,128)(2,1)} %param.12) | data formatting | bytes 3145728 | tf_op args[1]
  42.2 0.0 copy-done.6
  42.2 0.1 copy.17
  42.3 0.0 copy-done.7
  42.3 0.1 copy.16
  42.4 0.0 copy-done.8
  42.5 0.0 copy-done.5
  42.5 1.1 %fusion.13 = f32[1024,128]{1,0:T(8,128)} fusion(bf16[256,128]{1,0:T(8,128)(2,1)S(1)} %copy-done.5, bf16[1,1024,256]{2,1,0:T(8,128)(2,1)S(1)} %all-gather), kind=kOutput, calls=%fused_computation.34 | convolution fusion | flops 67108864 | bytes 1114112 | tf_op jit(solution)/shard_map/dot_general | solution.py:58
  43.6 0.0 copy-done.2
  43.6 0.0 copy-done.3
  43.6 8.9 %collective-permute-done.2 = bf16[1024,256]{1,0:T(8,128)(2,1)S(1)} collective-permute-done((bf16[1024,256]{1,0:T(8,128)(2,1)S(1)}, bf16[1024,256]{1,0:T(8,128)(2,1)S(1)}, u32[]{:S(2)}, u32[]{:S(2)}) %collective-permute-start.2) | collective-permute-done | bytes 524320 | tf_op jit(solution)/shard_map/ppermute | solution.py:18
  52.5 0.0 copy-start.4
  52.5 0.8 copy-done.4
  53.3 1.6 %pad_maximum_fusion = bf16[4,1024,256]{2,1,0:T(8,128)(2,1)S(1)} fusion(bf16[1,1024,256]{2,1,0:T(8,128)(2,1)} %bitcast.62, bf16[1,1024,256]{2,1,0:T(8,128)(2,1)} %bitcast.61, bf16[1,1024,256]{2,1,0:T(8,128)(2,1)} %bitcast.60, bf16[1,1024,256]{2,1,0:T(8,128)(2,1)S(1)} %all-gather), kind=kLoop, calls=%fused_computation.17 | loop fusion | flops 3145728 | bytes 4194304 | tf_op jit(solution)/shard_map/stack | solution.py:20
  54.9 2.0 %gather_fusion.1 = bf16[4,1024,256]{2,1,0:T(8,128)(2,1)} fusion(bf16[4,1024,256]{2,1,0:T(8,128)(2,1)S(1)} %pad_maximum_fusion, s32[1024]{0:T(1024)S(1)} %pad_clamp_fusion.1), kind=kCustom, calls=%fused_computation.1 | custom fusion | bytes 4194320 | tf_op jit(solution)/shard_map/gather | solution.py:20
  56.9 13.8 %while.14 = (s32[]{:T(128)}, f32[4,128,256]{2,1,0:T(8,128)S(1)}, s32[4,4]{0,1:T(4,128)S(1)}, bf16[4,4,3,128,128]{4,3,2,0,1:T(8,128)(2,1)}, bf16[4,8,128,256]{3,2...) while((s32[]{:T(128)}, f32[4,128,256]{2,1,0:T(8,128)S(1)}, ...), condition=%wide.region_1.2_spmd.clone, body=%wide.region_0.1_spmd.clone.sunk | while | flops 101123120 | bytes 4854835 | solution.py:55
  56.9 1.1 %dynamic-slice_bitcast_fusion.2 = bf16[8,128,256]{2,1,0:T(8,128)(2,1)S(1)} fusion(bf16[4,8,128,256]{3,2,1,0:T(8,128)(2,1)} %get-tuple-element.241, s32[]{:T(128)} %get-tuple-element.229), kind=kLoop, calls=%fused_computation.5.clone.1 | loop fusion | bytes 1048580 | tf_op jit(solution)/shard_map/while/body/eval_jaxpr/jit(dynamic_index_in_dim)/squeeze | solution.py:44
  58.1 0.1 copy.22
  58.2 0.1 reshape.158
  58.3 0.6 gather_fusion
  58.9 0.1 iota_compare_fusion.2
  59.0 1.4 %fusion.25 = f32[4,128,256]{2,1,0:T(8,128)S(1)} fusion(bf16[4,3,128,256]{3,2,1,0:T(8,128)(2,1)S(1)} %bitcast.56, f32[4,128,256]{2,1,0:T(8,128)S(1)} %get-tuple-element.230, bf16[4,4,3,128,128]{4,3,2,0,1:T(8,128)(2,1)} %get-tuple-element.240, s32[]{:T(128)} %get-tuple-element.229, pred[4,3]{1,0:T(4,128)(4,1)S(1)} %iota_compare_fusion.2, pred[]{:T(512)S(6)} %compare.10), kind=kOutput, calls=%fused_computation.4.clone.1 | convolution fusion | flops 101122048 | bytes 2228749 | tf_op jit(solution)/shard_map/while/body/eval_jaxpr/bcij,bcjf->bif/dot_general | solution.py:51
  60.4 1.1 dynamic-slice_bitcast_fusion.2
  61.5 0.1 copy.22
  61.6 0.1 reshape.158
  61.7 0.6 gather_fusion
  62.3 0.1 iota_compare_fusion.2
  62.4 1.4 %fusion.25 = f32[4,128,256]{2,1,0:T(8,128)S(1)} fusion(bf16[4,3,128,256]{3,2,1,0:T(8,128)(2,1)S(1)} %bitcast.56, f32[4,128,256]{2,1,0:T(8,128)S(1)} %get-tuple-element.230, bf16[4,4,3,128,128]{4,3,2,0,1:T(8,128)(2,1)} %get-tuple-element.240, s32[]{:T(128)} %get-tuple-element.229, pred[4,3]{1,0:T(4,128)(4,1)S(1)} %iota_compare_fusion.2, pred[]{:T(512)S(6)} %compare.10), kind=kOutput, calls=%fused_computation.4.clone.1 | convolution fusion | flops 101122048 | bytes 2228749 | tf_op jit(solution)/shard_map/while/body/eval_jaxpr/bcij,bcjf->bif/dot_general | solution.py:51
  63.9 1.1 dynamic-slice_bitcast_fusion.2
  65.0 0.1 copy.22
  65.1 0.1 reshape.158
  65.1 0.6 gather_fusion
  65.8 0.1 iota_compare_fusion.2
  65.8 1.4 %fusion.25 = f32[4,128,256]{2,1,0:T(8,128)S(1)} fusion(bf16[4,3,128,256]{3,2,1,0:T(8,128)(2,1)S(1)} %bitcast.56, f32[4,128,256]{2,1,0:T(8,128)S(1)} %get-tuple-element.230, bf16[4,4,3,128,128]{4,3,2,0,1:T(8,128)(2,1)} %get-tuple-element.240, s32[]{:T(128)} %get-tuple-element.229, pred[4,3]{1,0:T(4,128)(4,1)S(1)} %iota_compare_fusion.2, pred[]{:T(512)S(6)} %compare.10), kind=kOutput, calls=%fused_computation.4.clone.1 | convolution fusion | flops 101122048 | bytes 2228749 | tf_op jit(solution)/shard_map/while/body/eval_jaxpr/bcij,bcjf->bif/dot_general | solution.py:51
  67.3 1.1 dynamic-slice_bitcast_fusion.2
  68.4 0.1 copy.22
  68.5 0.1 reshape.158
  68.6 0.6 gather_fusion
  69.2 0.1 iota_compare_fusion.2
  69.3 1.4 %fusion.25 = f32[4,128,256]{2,1,0:T(8,128)S(1)} fusion(bf16[4,3,128,256]{3,2,1,0:T(8,128)(2,1)S(1)} %bitcast.56, f32[4,128,256]{2,1,0:T(8,128)S(1)} %get-tuple-element.230, bf16[4,4,3,128,128]{4,3,2,0,1:T(8,128)(2,1)} %get-tuple-element.240, s32[]{:T(128)} %get-tuple-element.229, pred[4,3]{1,0:T(4,128)(4,1)S(1)} %iota_compare_fusion.2, pred[]{:T(512)S(6)} %compare.10), kind=kOutput, calls=%fused_computation.4.clone.1 | convolution fusion | flops 101122048 | bytes 2228749 | tf_op jit(solution)/shard_map/while/body/eval_jaxpr/bcij,bcjf->bif/dot_general | solution.py:51
  70.7 0.0 copy-start.9
  70.7 0.0 copy-start.10
  70.7 0.1 fusion.9
  70.9 7.0 %all_gather.7 = bf16[1024,256]{1,0:T(8,128)(2,1)S(1)} all-gather(bf16[512,256]{1,0:T(8,128)(2,1)S(1)} %fusion.9), channel_id=1, replica_groups=mesh['row'=4,'replica'=4,'feat'=2] {'feat'}, dimensions={0}, use_global_device_ids=true | all-gather | bytes 786432 | tf_op jit(solution)/shard_map/all_gather | solution.py:57
  77.9 0.0 copy-done
  77.9 0.0 copy-done.1
  77.9 0.4 fusion.15
  78.3 29.5 %all-reduce = (f32[128]{0:T(128)S(1)}, f32[128]{0:T(128)S(1)}) all-reduce(f32[128]{0:T(128)S(1)} %get-tuple-element.166, f32[128]{0:T(128)S(1)} %get-tuple-element.165), channel_id=1, replica_groups=mesh['row'=4,'replica'=4,'feat'=2] {'row','replica'}, use_global_device_ids=true, to_apply=%region_5.6 | all-reduce | flops 256 | bytes 2048 | tf_op jit(solution)/shard_map/psum | solution.py:61
  107.8 0.0 copy-done.9
  107.8 0.0 copy-done.10
  107.8 0.8 fusion.10
  (18 shorter events, 0.2 us)
Async XLA Ops:
  0.0 77.9 %copy-start = (bf16[256,128]{1,0:T(8,128)(2,1)S(1)}, bf16[256,128]{1,0:T(8,128)(2,1)}, u32[]{:S(2)}) copy-start(bf16[256,128]{1,0:T(8,128)(2,1)} %param.17) | copy-start | bytes 196612
  0.0 42.2 %copy-start.6 = (s32[1,4,4,3]{2,1,3,0:T(4,128)S(1)}, s32[1,4,4,3]{2,1,3,0:T(4,128)}, u32[]{:S(2)}) copy-start(s32[1,4,4,3]{2,1,3,0:T(4,128)} %param.13) | copy-start | bytes 580
  0.0 42.3 %copy-start.7 = (s32[1,4,4]{2,1,0:T(4,128)S(1)}, s32[1,4,4]{2,1,0:T(4,128)}, u32[]{:S(2)}) copy-start(s32[1,4,4]{2,1,0:T(4,128)} %param.14) | copy-start | bytes 196
  0.0 42.4 %copy-start.8 = (s32[1,512]{1,0:T(1,128)S(1)}, s32[1,512]{1,0:T(1,128)}, u32[]{:S(2)}) copy-start(s32[1,512]{1,0:T(1,128)} %param.15) | copy-start | bytes 6148
  0.0 42.4 %copy-start.5 = (bf16[256,128]{1,0:T(8,128)(2,1)S(1)}, bf16[256,128]{1,0:T(8,128)(2,1)}, u32[]{:S(2)}) copy-start(bf16[256,128]{1,0:T(8,128)(2,1)} %param.16) | copy-start | bytes 196612
  10.4 14.9 %collective-permute-start = (bf16[1024,256]{1,0:T(8,128)(2,1)S(1)}, bf16[1024,256]{1,0:T(8,128)(2,1)S(1)}, u32[]{:S(2)}, u32[]{:S(2)}) collective-permute-start(bf16[1024,256]{1,0:T(8,128)(2,1)S(1)} %bitcast.59), channel_id=1, source_target_pairs={{0,8},{8,16},{16,24},{24,0},{1,9},{9,17},{17,25},{25,1},{2,10},{10... | collective-permute-start | bytes 1572872 | tf_op jit(solution)/shard_map/ppermute | solution.py:18
  25.3 18.3 %copy-start.2 = (bf16[1024,256]{1,0:T(8,128)(2,1)}, bf16[1024,256]{1,0:T(8,128)(2,1)S(1)}, u32[]{:S(2)}) copy-start(bf16[1024,256]{1,0:T(8,128)(2,1)S(1)} %collective-permute-done) | copy-start | bytes 1572868
  25.3 14.0 %collective-permute-start.1 = (bf16[1024,256]{1,0:T(8,128)(2,1)S(1)}, bf16[1024,256]{1,0:T(8,128)(2,1)S(1)}, u32[]{:S(2)}, u32[]{:S(2)}) collective-permute-start(bf16[1024,256]{1,0:T(8,128)(2,1)S(1)} %collective-permute-done), channel_id=1, source_target_pairs={{0,8},{8,16},{16,24},{24,0},{1,9},{9,17},{17,25},{25,1},{2,10},{10... | collective-permute-start | bytes 1572872 | tf_op jit(solution)/shard_map/ppermute | solution.py:18
  39.3 4.3 %copy-start.3 = (bf16[1024,256]{1,0:T(8,128)(2,1)}, bf16[1024,256]{1,0:T(8,128)(2,1)S(1)}, u32[]{:S(2)}) copy-start(bf16[1024,256]{1,0:T(8,128)(2,1)S(1)} %collective-permute-done.1) | copy-start | bytes 1572868
  39.3 13.2 %collective-permute-start.2 = (bf16[1024,256]{1,0:T(8,128)(2,1)S(1)}, bf16[1024,256]{1,0:T(8,128)(2,1)S(1)}, u32[]{:S(2)}, u32[]{:S(2)}) collective-permute-start(bf16[1024,256]{1,0:T(8,128)(2,1)S(1)} %collective-permute-done.1), channel_id=1, source_target_pairs={{0,8},{8,16},{16,24},{24,0},{1,9},{9,17},{17,25},{25,1},{2,10},{10... | collective-permute-start | bytes 1572872 | tf_op jit(solution)/shard_map/ppermute | solution.py:18
  52.5 0.8 copy-start.4
  56.9 21.0 %copy-start.1 = (f32[1024,128]{1,0:T(8,128)S(1)}, f32[1024,128]{1,0:T(8,128)}, u32[]{:S(2)}) copy-start(f32[1024,128]{1,0:T(8,128)} %fusion.13) | copy-start | bytes 1572868
  70.7 37.1 %copy-start.9 = (f32[128]{0:T(128)S(1)}, f32[128]{0:T(128)}, u32[]{:S(2)}) copy-start(f32[128]{0:T(128)} %param.19) | copy-start | bytes 1540
  70.7 37.1 %copy-start.10 = (f32[128]{0:T(128)S(1)}, f32[128]{0:T(128)}, u32[]{:S(2)}) copy-start(f32[128]{0:T(128)} %param.18) | copy-start | bytes 1540
